TPU v7x, 32 devices: a whole 2x2x4 slice. The times are simulated.
32 devices in a mesh: ctx: 8 (over z, x), head: 4 (over y, core).
Axes of the slice: x: 2, y: 2, z: 4, core: 2. Of those that a mesh axis runs over, the one named last changes fastest.
Arguments:
- query_nope: bfloat16 [256, 16384], P('head'), may hold values from -6 to 6
- query_rope: bfloat16 [256, 8192], P('head'), may hold values from -10 to 10
- latent_cache: bfloat16 [4096, 512], P('ctx'), may hold values from -6 to 6
- rope_keys: bfloat16 [64, 4096], P(None, 'ctx'), may hold values from -6 to 6
- absorb_keys: bfloat16 [128, 128, 512], P('head'), may hold values from -0.5 to 0.5
- expand_values: bfloat16 [128, 512, 128], P('head'), may hold values from -2.09375 to 2.09375
- block_ids: int32 [128, 2, 16], P('head'), may hold values from -1 to 31, as said below
- block_counts: int32 [128, 2], P('head'), may hold values from 8 to 16
Outputs:
- attended: bfloat16 [256, 16384], P('head')
Inputs may be any that keep to these rules, and one draw needn't show every extreme that they name: `block_ids`: entries beyond block_counts are -1; the first block_counts entries are distinct blocks, none after the query block's own block 30 + q, and entry 0 is that own block.
All inputs are finite; a program needn't handle non-finite values.
Results may differ from a plain program's by a relative error of at most 0.0066.
Values may be sent and summed in bfloat16 or wider, within the bound.
No kernel may reach another device: no remote copies, remote signals or barrier semaphores. Data moves between devices by JAX's collectives and lax.ppermute only.
A program may use at most 128 MiB of HBM per device.

v0:
```python
import math
import jax
import jax.numpy as jnp
from jax import lax
from jax.sharding import PartitionSpec as P

BLOCK = 128


def body(
    query_nope,
    query_rope,
    latent_cache,
    rope_keys,
    absorb_keys,
    expand_values,
    block_ids,
    block_counts,
):
    nope_all, rope_all = (
        lax.all_to_all(query_nope, "head", split_axis=1, concat_axis=0, tiled=True),
        lax.all_to_all(query_rope, "head", split_axis=1, concat_axis=0, tiled=True),
    )
    tokens = nope_all.shape[0]
    heads_here = absorb_keys.shape[0]
    nope_width = absorb_keys.shape[1]
    rope_width = rope_keys.shape[0]
    value_width = expand_values.shape[2]
    keys_here = latent_cache.shape[0]
    blocks_here = keys_here // BLOCK
    query_blocks = tokens // BLOCK
    slot_count = block_ids.shape[2]
    shards = lax.axis_size("ctx")
    ctx_index = lax.axis_index("ctx")
    score_scale = 1.0 / math.sqrt(nope_width + rope_width)
    query_latent = jnp.einsum(
        "thn,hnl->htl",
        nope_all.reshape(tokens, heads_here, nope_width),
        absorb_keys,
        preferred_element_type=jnp.float32,
    ).astype(jnp.bfloat16)
    scores = jnp.einsum(
        "htl,kl->htk", query_latent, latent_cache, preferred_element_type=jnp.float32
    )
    scores = scores + jnp.einsum(
        "thr,rk->htk",
        rope_all.reshape(tokens, heads_here, rope_width),
        rope_keys,
        preferred_element_type=jnp.float32,
    )
    scores = (scores * score_scale).reshape(heads_here, query_blocks, BLOCK, blocks_here, BLOCK)
    block_global = ctx_index * blocks_here + jnp.arange(blocks_here, dtype=jnp.int32)
    slot_live = jnp.arange(slot_count, dtype=jnp.int32)[None, None, :] < block_counts[:, :, None]
    chosen = jnp.any((block_ids[..., None] == block_global) & slot_live[..., None], axis=2)
    query_pos = keys_here * shards - tokens + jnp.arange(tokens, dtype=jnp.int32)
    key_pos = ctx_index * keys_here + jnp.arange(keys_here, dtype=jnp.int32)
    causal = (key_pos[None, :] <= query_pos[:, None]).reshape(
        query_blocks, BLOCK, blocks_here, BLOCK
    )
    allowed = chosen[:, :, None, :, None] & causal[None]
    local_top = jnp.max(jnp.where(allowed, scores, -1e30), axis=(3, 4))
    weights = jnp.where(allowed, jnp.exp(scores - local_top[..., None, None]), 0.0).astype(
        jnp.bfloat16
    )
    weights = weights.reshape(heads_here, tokens, keys_here)
    top_rows = local_top.reshape(heads_here, tokens).T
    weight_total = jnp.sum(weights, axis=2, dtype=jnp.float32).T
    latent_sum = jnp.einsum(
        "htk,kl->thl", weights, latent_cache, preferred_element_type=jnp.float32
    )
    value_float = expand_values.astype(jnp.float32)
    per_device = tokens // shards
    partial_out = jnp.einsum(
        "thl,hlv->thv", latent_sum, value_float, precision=lax.Precision.HIGHEST
    )
    parts_out, parts_total, parts_top = (
        lax.all_to_all(partial_out[None], "ctx", split_axis=1, concat_axis=0, tiled=True),
        lax.all_to_all(weight_total[None], "ctx", split_axis=1, concat_axis=0, tiled=True),
        lax.all_to_all(top_rows[None], "ctx", split_axis=1, concat_axis=0, tiled=True),
    )
    best = jnp.max(parts_top, axis=0)
    factor = jnp.exp(parts_top - best[None])
    summed_out = jnp.sum(parts_out * factor[..., None], axis=0)
    summed_total = jnp.sum(parts_total * factor, axis=0)
    rows_done = (
        (summed_out / summed_total[..., None])
        .astype(jnp.bfloat16)
        .reshape(per_device, heads_here * value_width)
    )
    merged = lax.all_gather(rows_done, "ctx", axis=0, tiled=True)
    return lax.all_to_all(merged, "head", split_axis=0, concat_axis=1, tiled=True)


def solution(mesh):
    return jax.shard_map(
        body,
        mesh=mesh,
        in_specs=(
            P("head", None),
            P("head", None),
            P("ctx", None),
            P(None, "ctx"),
            P("head", None, None),
            P("head", None, None),
            P("head", None, None),
            P("head", None),
        ),
        out_specs=P("head", None),
        check_vma=False,
    )
```

profile of v0, /device:TPU:0, one launch (start us, length us, event | category | flops | bytes accessed | tf_op | source)
XLA Modules:
  0.0 328.8 jit_solution(10380978903736725854)
XLA Ops:
  6.5 2.4 copy.105
  8.9 4.3 %all-to-all-start.1 = ((bf16[64,4,2048]{2,0,1:T(8,128)(2,1)}), bf16[64,4,2048]{2,0,1:T(8,128)(2,1)S(1)}, u32[]{:S(2)}, u32[]{:S(2)}) async-start(bf16[64,4,2048]{2,0,1:T(8,128)(2,1)} %bitcast.63), calls=%async_computation.1 | async-start | bytes 2097152 | tf_op jit(solution)/shard_map/all_to_all | solution.py:22
  13.2 3.2 copy.104
  16.3 11.3 %all-to-all-done.1 = bf16[64,4,2048]{2,0,1:T(8,128)(2,1)S(1)} async-done(((bf16[64,4,2048]{2,0,1:T(8,128)(2,1)}), bf16[64,4,2048]{2,0,1:T(8,128)(2,1)S(1)}, u32[]{:S(2)}, u32[]{:S(2)}) %all-to-all-start.1) | async-done | bytes 1048608 | tf_op jit(solution)/shard_map/all_to_all | solution.py:22
  27.6 4.4 %all-to-all-start = ((bf16[64,4,4096]{2,0,1:T(8,128)(2,1)}), bf16[64,4,4096]{2,0,1:T(8,128)(2,1)}, u32[]{:S(2)}, u32[]{:S(2)}) async-start(bf16[64,4,4096]{2,0,1:T(8,128)(2,1)} %bitcast.62), calls=%async_computation | async-start | bytes 4194304 | tf_op jit(solution)/shard_map/all_to_all | solution.py:21
  32.3 4.2 %and.28 = pred[32,2,128,4,128]{4,3,2,1,0:T(4,128)(4,1)} broadcast(pred[32,2,4]{2,1,0:T(4,128)(4,1)S(1)} %copy.70), dimensions={0,1,3} | broadcast | bytes 4194560 | tf_op jit(solution)/shard_map/and | solution.py:60
  36.5 14.4 %and.29 = pred[32,256,512]{2,1,0:T(32,128)(4,1)} reshape(pred[32,2,128,4,128]{4,3,2,1,0:T(4,128)(4,1)} %and.28) | data formatting | bytes 8388608 | tf_op jit(solution)/shard_map/and | solution.py:60
  51.0 3.3 %reshape.108 = bf16[256,32,64]{2,1,0:T(8,128)(2,1)S(1)} reshape(bf16[4,64,2048]{2,1,0:T(8,128)(2,1)} %bitcast.66) | data formatting | bytes 2097152 | tf_op jit(solution)/shard_map/reshape | solution.py:47
  54.4 8.0 %fusion.10 = f32[512,256,32]{0,1,2:T(8,128)} fusion(bf16[256,32,64]{2,1,0:T(8,128)(2,1)S(1)} %reshape.108, bf16[64,512]{1,0:T(8,128)(2,1)S(1)} %copy-done.3), kind=kOutput, calls=%fused_computation.13 | convolution fusion | flops 536870912 | bytes 17891328 | tf_op jit(solution)/shard_map/thr,rk->htk/dot_general | solution.py:45
  62.4 2.1 copy.90
  64.5 17.7 %select_reduce_fusion = (f32[32,256]{1,0:T(8,128)S(1)}, f32[32,256,512]{2,1,0:T(8,128)}) fusion(pred[32,256,512]{2,1,0:T(32,128)(4,1)} %and.29, pred[256,512]{1,0:T(8,128)(4,1)S(1)} %broadcast_compare_fusion, f32[512,256,32]{0,1,2:T(8,128)} %fusion.10, bf16[512,512]{1,0:T(8,128)(2,1)S(1)} %copy-done, bf16[32,128,512]{2,1,0:T(8,128)(2,1)} %param.12, ...), kind=kOutput, calls=%fused_computation.6 | convolution fusion | flops 5393866752 | bytes 44728320 | tf_op jit(solution)/shard_map/htl,kl->htk/dot_general | solution.py:42
  82.2 9.9 %convert_reduce_fusion = f32[32,256]{1,0:T(8,128)S(1)} fusion(f32[32,256,512]{2,1,0:T(8,128)} %get-tuple-element.8, f32[32,256]{1,0:T(8,128)S(1)} %get-tuple-element.7, pred[32,256,512]{2,1,0:T(32,128)(4,1)} %and.29, pred[256,512]{1,0:T(8,128)(4,1)S(1)} %broadcast_compare_fusion), kind=kLoop, calls=%fused_computation.4 | loop fusion | flops 25157632 | bytes 21168128 | tf_op jit(solution)/shard_map/reduce_sum | solution.py:67
  92.1 0.5 broadcast.83
  92.7 0.9 reduce.1
  93.6 0.7 reshape.113
  94.4 6.5 %all-to-all-start.4 = ((f32[8,1,1024]{2,1,0:T(1,128)}), f32[8,1,1024]{2,1,0:T(1,128)S(1)}, u32[]{:S(2)}, u32[]{:S(2)}) async-start(f32[8,1,1024]{2,1,0:T(1,128)} %reshape.113), calls=%async_computation.4 | async-start | bytes 65536 | tf_op jit(solution)/shard_map/all_to_all | solution.py:78
  100.9 12.9 %fusion.14 = f32[32,256,512]{2,1,0:T(8,128)} fusion(bf16[512,512]{1,0:T(8,128)(2,1)S(1)} %copy-done, f32[32,256,512]{2,1,0:T(8,128)} %get-tuple-element.8, pred[32,256,512]{2,1,0:T(32,128)(4,1)} %and.29, f32[32,256]{1,0:T(8,128)S(1)} %get-tuple-element.7, pred[256,512]{1,0:T(8,128)(4,1)S(1)} %broadcast_compare_fusion), kind=kOutput, calls=%fused_computation.17 | convolution fusion | flops 4311744512 | bytes 38436864 | tf_op jit(solution)/shard_map/htk,kl->thl/dot_general | solution.py:68
  113.8 0.9 reduce.3
  114.8 0.7 reshape.111
  115.5 6.0 %all-to-all-start.3 = ((f32[8,1,1024]{2,1,0:T(1,128)}), f32[8,1,1024]{2,1,0:T(1,128)S(1)}, u32[]{:S(2)}, u32[]{:S(2)}) async-start(f32[8,1,1024]{2,1,0:T(1,128)} %reshape.111), calls=%async_computation.3 | async-start | bytes 65536 | tf_op jit(solution)/shard_map/all_to_all | solution.py:79
  121.5 13.2 %fusion.7 = f32[1,256,32,128]{3,1,2,0:T(8,128)S(1)} fusion(bf16[32,512,128]{2,1,0:T(8,128)(2,1)} %param.13, f32[32,256,512]{2,1,0:T(8,128)} %fusion.14), kind=kOutput, calls=%fused_computation.11 | convolution fusion | flops 6442450944 | bytes 25165824 | tf_op jit(solution)/shard_map/thl,hlv->thv/dot_general | solution.py:73
  134.7 4.4 %copy.76 = f32[1,256,32,128]{3,2,0,1:T(8,128)} copy(f32[1,256,32,128]{3,1,2,0:T(8,128)S(1)} %fusion.7) | data formatting | bytes 8388608 | tf_op jit(solution)/shard_map/broadcast_in_dim | solution.py:77
  139.1 6.0 %all-to-all-start.2 = ((f32[1,256,32,128]{3,2,0,1:T(8,128)}), f32[1,256,32,128]{3,2,0,1:T(8,128)}, u32[]{:S(2)}, u32[]{:S(2)}) async-start(f32[1,256,32,128]{3,2,0,1:T(8,128)} %copy.76), calls=%async_computation.2 | async-start | bytes 8388608 | tf_op jit(solution)/shard_map/all_to_all | solution.py:77
  145.1 0.7 reduce.2
  146.2 0.7 reduce.4
  146.9 0.2 reshape.112
  147.4 90.5 %all-to-all-done.2 = f32[1,256,32,128]{3,2,0,1:T(8,128)} async-done(((f32[1,256,32,128]{3,2,0,1:T(8,128)}), f32[1,256,32,128]{3,2,0,1:T(8,128)}, u32[]{:S(2)}, u32[]{:S(2)}) %all-to-all-start.2) | async-done | bytes 4194336 | tf_op jit(solution)/shard_map/all_to_all | solution.py:77
  237.8 3.9 %fusion.6 = f32[32,32,128]{2,0,1:T(8,128)S(1)} fusion(f32[8,32,32,128]{3,2,1,0:T(8,128)} %bitcast.10, f32[8,32,32]{1,0,2:T(8,128)S(1)} %get-tuple-element.6), kind=kLoop, calls=%fused_computation.10 | loop fusion | flops 1966080 | bytes 4751360 | tf_op jit(solution)/shard_map/reduce_sum | solution.py:83
  241.8 0.9 copy_bitcast_fusion.2
  242.7 48.4 %all-gather.2.cloned.1.call-done = bf16[256,4096]{1,0:T(8,128)(2,1)} async-done(((bf16[32,4096]{1,0:T(8,128)(2,1)}), bf16[256,4096]{1,0:T(8,128)(2,1)}) %all-gather.2.cloned.1.call-update) | async-done | bytes 2097168 | tf_op jit(solution)/shard_map/all_gather | solution.py:90
  291.2 29.4 %all_to_all.87 = bf16[4,64,4096]{2,1,0:T(8,128)(2,1)S(1)} all-to-all(bf16[4,64,4096]{2,1,0:T(8,128)(2,1)} %bitcast.68), channel_id=1, replica_groups=mesh['ctx'=8,'head'=4] {'head'}, dimensions={0} | all-to-all | bytes 4194304 | tf_op jit(solution)/shard_map/all_to_all | solution.py:91
  320.5 1.5 copy.89
  (32 shorter events, 1.3 us)
Async XLA Ops:
  6.5 58.0 %copy-start = (bf16[512,512]{1,0:T(8,128)(2,1)S(1)}, bf16[512,512]{1,0:T(8,128)(2,1)}, u32[]{:S(2)}) copy-start(bf16[512,512]{1,0:T(8,128)(2,1)} %param.10) | copy-start | bytes 1572868
  8.9 18.7 %all-to-all-start.1 = ((bf16[64,4,2048]{2,0,1:T(8,128)(2,1)}), bf16[64,4,2048]{2,0,1:T(8,128)(2,1)S(1)}, u32[]{:S(2)}, u32[]{:S(2)}) async-start(bf16[64,4,2048]{2,0,1:T(8,128)(2,1)} %bitcast.63), calls=%async_computation.1 | async-start | bytes 2097152 | tf_op jit(solution)/shard_map/all_to_all | solution.py:22
  13.2 18.9 %copy-start.5 = (s32[32,2]{0,1:T(2,128)S(1)}, s32[32,2]{0,1:T(2,128)}, u32[]{:S(2)}) copy-start(s32[32,2]{0,1:T(2,128)} %param.15) | copy-start | bytes 772
  13.2 18.9 %copy-start.4 = (s32[32,2,16]{0,2,1:T(8,128)S(1)}, s32[32,2,16]{0,2,1:T(8,128)}, u32[]{:S(2)}) copy-start(s32[32,2,16]{0,2,1:T(8,128)} %param.14) | copy-start | bytes 12292
  27.6 8.9 %copy-start.2 = (bf16[64,4,2048]{2,0,1:T(8,128)(2,1)}, bf16[64,4,2048]{2,0,1:T(8,128)(2,1)S(1)}, u32[]{:S(2)}) copy-start(bf16[64,4,2048]{2,0,1:T(8,128)(2,1)S(1)} %all-to-all-done.1) | copy-start | bytes 3145732
  27.6 34.8 %all-to-all-start = ((bf16[64,4,4096]{2,0,1:T(8,128)(2,1)}), bf16[64,4,4096]{2,0,1:T(8,128)(2,1)}, u32[]{:S(2)}, u32[]{:S(2)}) async-start(bf16[64,4,4096]{2,0,1:T(8,128)(2,1)} %bitcast.62), calls=%async_computation | async-start | bytes 4194304 | tf_op jit(solution)/shard_map/all_to_all | solution.py:21
  36.5 17.9 %copy-start.3 = (bf16[64,512]{1,0:T(8,128)(2,1)S(1)}, bf16[64,512]{1,0:T(8,128)(2,1)}, u32[]{:S(2)}) copy-start(bf16[64,512]{1,0:T(8,128)(2,1)} %param.11) | copy-start | bytes 196612
  94.4 21.2 %all-to-all-start.4 = ((f32[8,1,1024]{2,1,0:T(1,128)}), f32[8,1,1024]{2,1,0:T(1,128)S(1)}, u32[]{:S(2)}, u32[]{:S(2)}) async-start(f32[8,1,1024]{2,1,0:T(1,128)} %reshape.113), calls=%async_computation.4 | async-start | bytes 65536 | tf_op jit(solution)/shard_map/all_to_all | solution.py:78
  115.5 23.6 %all-to-all-start.3 = ((f32[8,1,1024]{2,1,0:T(1,128)}), f32[8,1,1024]{2,1,0:T(1,128)S(1)}, u32[]{:S(2)}, u32[]{:S(2)}) async-start(f32[8,1,1024]{2,1,0:T(1,128)} %reshape.111), calls=%async_computation.3 | async-start | bytes 65536 | tf_op jit(solution)/shard_map/all_to_all | solution.py:79
  139.1 98.8 %all-to-all-start.2 = ((f32[1,256,32,128]{3,2,0,1:T(8,128)}), f32[1,256,32,128]{3,2,0,1:T(8,128)}, u32[]{:S(2)}, u32[]{:S(2)}) async-start(f32[1,256,32,128]{3,2,0,1:T(8,128)} %copy.76), calls=%async_computation.2 | async-start | bytes 8388608 | tf_op jit(solution)/shard_map/all_to_all | solution.py:77
  145.1 146.1 %all-gather.2.cloned.1.call-start = ((), (), s32[]{:S(2)}) async-start(), calls=%async_computation.6 | async-start | bytes 2359296 | tf_op jit(solution)/shard_map/all_gather | solution.py:90
  291.2 30.8 %copy-start.1 = (bf16[512,512]{1,0:T(8,128)(2,1)S(1)}, bf16[512,512]{1,0:T(8,128)(2,1)}, u32[]{:S(2)}) copy-start(bf16[512,512]{1,0:T(8,128)(2,1)} %param.10) | copy-start | bytes 1572868
Sparse Core Ops, SparseCore 0:
  242.8 48.2 all-gather.1
where the time goes:
time: 330 us; the launch traced here: 329 us
  waiting for transfers between devices  150 us (45%)
  matrix products  51.8 us (16%)
  local copies, waits for them, and re-layouts  38.3 us (12%)
  blocking collectives  29.4 us (9%)
  starting transfers between devices  27.2 us (8%)
  other arithmetic  18.3 us (6%)
  between operations  13.6 us (4%)
    all_to_all x1, waiting for transfers between devices, body(): lax.all_to_all(partial_out[None], 'ctx', split_axis=1, concat_axis=0, til...  90.5 us
    all_gather x1, waiting for transfers between devices, body(): merged = lax.all_gather(rows_done, 'ctx', axis=0, tiled=True)  48.4 us
    all_to_all x1, blocking collectives, body(): lax.all_to_all(merged, 'head', split_axis=0, concat_axis=1, tiled=True)  29.4 us
    and x2, local copies, waits for them, and re-layouts, body(): allowed = chosen[:, :, None, :, None] & causal[None]  18.5 us
    dot_general x1, matrix products, body(): jnp.einsum('htl,kl->htk', query_latent, latent_cache, preferred_element_t...  17.7 us
    dot_general x1, matrix products, body(): jnp.einsum('thl,hlv->thv', latent_sum, value_float, precision=lax.Precisi...  13.2 us
    dot_general x1, matrix products, body(): jnp.einsum('htk,kl->thl', weights, latent_cache, preferred_element_type=j...  12.9 us
    all_to_all x1, waiting for transfers between devices, body(): lax.all_to_all(query_rope, 'head', split_axis=1, concat_axis=0, tiled=True)  11.3 us
  transfers between devices with their start and end apart: 6, of which 3 were waited for; matrix products, arithmetic and copies ran while one was open for 21% of the time, Pallas kernels for 0%

commit v1 on v0

--- a/solution.py
+++ b/solution.py
@@ -87,7 +87,10 @@
         .astype(jnp.bfloat16)
         .reshape(per_device, heads_here * value_width)
     )
-    merged = lax.all_gather(rows_done, "ctx", axis=0, tiled=True)
+    built = lax.axis_size("ctx")
+    arr_next = jnp.stack([rows_done] * built)
+    wide_out = lax.all_to_all(arr_next, "ctx", 0, 0)
+    merged = jnp.concatenate(wide_out, axis=0)
     return lax.all_to_all(merged, "head", split_axis=0, concat_axis=1, tiled=True)
 
 

time: 330 us -> 319 us (0.967)
  blocking collectives: 29.4 us -> 80.3 us
  waiting for transfers between devices: 150 us -> 102 us
  between operations: 13.6 us -> 0.22 us
    all_to_all x0 -> x1, blocking collectives: none -> 51.8 us  [body(): wide_out = lax.all_to_all(arr_next, 'ctx', 0, 0)]
    all_gather x1 -> x0, waiting for transfers between devices: 48.4 us -> none  [body(): merged = lax.all_gather(rows_done, 'ctx', axis=0, tiled=True)]
  transfers between devices with their start and end apart: 6 -> 5, of which waited for: 3 -> 2; matrix products, arithmetic and copies ran while one was open for 21% -> 21% of each run, Pallas kernels for 0% -> 0%
where the time goes in v1:
time: 319 us; the launch traced here: 317 us
  waiting for transfers between devices  102 us (32%)
  blocking collectives  80.3 us (25%)
  matrix products  51.8 us (16%)
  local copies, waits for them, and re-layouts  38.5 us (12%)
  starting transfers between devices  27.2 us (9%)
  other arithmetic  17.6 us (6%)
    all_to_all x1, waiting for transfers between devices, body(): lax.all_to_all(partial_out[None], 'ctx', split_axis=1, concat_axis=0, til...  90.5 us
    all_to_all x1, blocking collectives, body(): wide_out = lax.all_to_all(arr_next, 'ctx', 0, 0)  51.8 us
    all_to_all x1, blocking collectives, body(): lax.all_to_all(merged, 'head', split_axis=0, concat_axis=1, tiled=True)  28.5 us
    and x2, local copies, waits for them, and re-layouts, body(): allowed = chosen[:, :, None, :, None] & causal[None]  18.5 us
    dot_general x1, matrix products, body(): jnp.einsum('htl,kl->htk', query_latent, latent_cache, preferred_element_t...  17.7 us
    dot_general x1, matrix products, body(): jnp.einsum('thl,hlv->thv', latent_sum, value_float, precision=lax.Precisi...  13.2 us
    dot_general x1, matrix products, body(): jnp.einsum('htk,kl->thl', weights, latent_cache, preferred_element_type=j...  12.9 us
    all_to_all x1, waiting for transfers between devices, body(): lax.all_to_all(query_rope, 'head', split_axis=1, concat_axis=0, tiled=True)  11.3 us
  transfers between devices with their start and end apart: 5, of which 2 were waited for; matrix products, arithmetic and copies ran while one was open for 21% of the time, Pallas kernels for 0%

profile of v1, /device:TPU:0, one launch (start us, length us, event | category | flops | bytes accessed | tf_op | source)
XLA Modules:
  0.0 317.4 jit_solution(9672299922645989118)
XLA Ops:
  0.0 2.4 copy.105
  2.4 4.3 %all-to-all-start.1 = ((bf16[64,4,2048]{2,0,1:T(8,128)(2,1)}), bf16[64,4,2048]{2,0,1:T(8,128)(2,1)S(1)}, u32[]{:S(2)}, u32[]{:S(2)}) async-start(bf16[64,4,2048]{2,0,1:T(8,128)(2,1)} %bitcast.63), calls=%async_computation.1 | async-start | bytes 2097152 | tf_op jit(solution)/shard_map/all_to_all | solution.py:22
  6.7 3.2 copy.104
  9.8 11.3 %all-to-all-done.1 = bf16[64,4,2048]{2,0,1:T(8,128)(2,1)S(1)} async-done(((bf16[64,4,2048]{2,0,1:T(8,128)(2,1)}), bf16[64,4,2048]{2,0,1:T(8,128)(2,1)S(1)}, u32[]{:S(2)}, u32[]{:S(2)}) %all-to-all-start.1) | async-done | bytes 1048608 | tf_op jit(solution)/shard_map/all_to_all | solution.py:22
  21.1 4.4 %all-to-all-start = ((bf16[64,4,4096]{2,0,1:T(8,128)(2,1)}), bf16[64,4,4096]{2,0,1:T(8,128)(2,1)}, u32[]{:S(2)}, u32[]{:S(2)}) async-start(bf16[64,4,4096]{2,0,1:T(8,128)(2,1)} %bitcast.62), calls=%async_computation | async-start | bytes 4194304 | tf_op jit(solution)/shard_map/all_to_all | solution.py:21
  25.8 4.2 %and.28 = pred[32,2,128,4,128]{4,3,2,1,0:T(4,128)(4,1)} broadcast(pred[32,2,4]{2,1,0:T(4,128)(4,1)S(1)} %copy.70), dimensions={0,1,3} | broadcast | bytes 4194560 | tf_op jit(solution)/shard_map/and | solution.py:60
  30.0 14.4 %and.29 = pred[32,256,512]{2,1,0:T(32,128)(4,1)} reshape(pred[32,2,128,4,128]{4,3,2,1,0:T(4,128)(4,1)} %and.28) | data formatting | bytes 8388608 | tf_op jit(solution)/shard_map/and | solution.py:60
  44.5 3.3 %reshape.112 = bf16[256,32,64]{2,1,0:T(8,128)(2,1)S(1)} reshape(bf16[4,64,2048]{2,1,0:T(8,128)(2,1)} %bitcast.67) | data formatting | bytes 2097152 | tf_op jit(solution)/shard_map/reshape | solution.py:47
  47.9 8.0 %fusion.10 = f32[512,256,32]{0,1,2:T(8,128)} fusion(bf16[256,32,64]{2,1,0:T(8,128)(2,1)S(1)} %reshape.112, bf16[64,512]{1,0:T(8,128)(2,1)S(1)} %copy-done.3), kind=kOutput, calls=%fused_computation.13 | convolution fusion | flops 536870912 | bytes 17891328 | tf_op jit(solution)/shard_map/thr,rk->htk/dot_general | solution.py:45
  55.9 2.1 copy.90
  58.0 17.7 %select_reduce_fusion = (f32[32,256]{1,0:T(8,128)S(1)}, f32[32,256,512]{2,1,0:T(8,128)}) fusion(pred[32,256,512]{2,1,0:T(32,128)(4,1)} %and.29, pred[256,512]{1,0:T(8,128)(4,1)S(1)} %broadcast_compare_fusion, f32[512,256,32]{0,1,2:T(8,128)} %fusion.10, bf16[512,512]{1,0:T(8,128)(2,1)S(1)} %copy-done, bf16[32,128,512]{2,1,0:T(8,128)(2,1)} %param.12, ...), kind=kOutput, calls=%fused_computation.6 | convolution fusion | flops 5393866752 | bytes 44728320 | tf_op jit(solution)/shard_map/htl,kl->htk/dot_general | solution.py:42
  75.7 9.9 %convert_reduce_fusion = f32[32,256]{1,0:T(8,128)S(1)} fusion(f32[32,256,512]{2,1,0:T(8,128)} %get-tuple-element.8, f32[32,256]{1,0:T(8,128)S(1)} %get-tuple-element.7, pred[32,256,512]{2,1,0:T(32,128)(4,1)} %and.29, pred[256,512]{1,0:T(8,128)(4,1)S(1)} %broadcast_compare_fusion), kind=kLoop, calls=%fused_computation.4 | loop fusion | flops 25157632 | bytes 21168128 | tf_op jit(solution)/shard_map/reduce_sum | solution.py:67
  85.6 0.5 broadcast.85
  86.2 0.9 reduce.1
  87.1 0.7 reshape.117
  87.8 6.5 %all-to-all-start.4 = ((f32[8,1,1024]{2,1,0:T(1,128)}), f32[8,1,1024]{2,1,0:T(1,128)S(1)}, u32[]{:S(2)}, u32[]{:S(2)}) async-start(f32[8,1,1024]{2,1,0:T(1,128)} %reshape.117), calls=%async_computation.4 | async-start | bytes 65536 | tf_op jit(solution)/shard_map/all_to_all | solution.py:78
  94.3 12.9 %fusion.14 = f32[32,256,512]{2,1,0:T(8,128)} fusion(bf16[512,512]{1,0:T(8,128)(2,1)S(1)} %copy-done, f32[32,256,512]{2,1,0:T(8,128)} %get-tuple-element.8, pred[32,256,512]{2,1,0:T(32,128)(4,1)} %and.29, f32[32,256]{1,0:T(8,128)S(1)} %get-tuple-element.7, pred[256,512]{1,0:T(8,128)(4,1)S(1)} %broadcast_compare_fusion), kind=kOutput, calls=%fused_computation.17 | convolution fusion | flops 4311744512 | bytes 38436864 | tf_op jit(solution)/shard_map/htk,kl->thl/dot_general | solution.py:68
  107.3 0.9 reduce.3
  108.3 0.7 reshape.115
  109.0 6.0 %all-to-all-start.3 = ((f32[8,1,1024]{2,1,0:T(1,128)}), f32[8,1,1024]{2,1,0:T(1,128)S(1)}, u32[]{:S(2)}, u32[]{:S(2)}) async-start(f32[8,1,1024]{2,1,0:T(1,128)} %reshape.115), calls=%async_computation.3 | async-start | bytes 65536 | tf_op jit(solution)/shard_map/all_to_all | solution.py:79
  115.0 13.2 %fusion.7 = f32[1,256,32,128]{3,1,2,0:T(8,128)S(1)} fusion(bf16[32,512,128]{2,1,0:T(8,128)(2,1)} %param.13, f32[32,256,512]{2,1,0:T(8,128)} %fusion.14), kind=kOutput, calls=%fused_computation.11 | convolution fusion | flops 6442450944 | bytes 25165824 | tf_op jit(solution)/shard_map/thl,hlv->thv/dot_general | solution.py:73
  128.2 4.4 %copy.76 = f32[1,256,32,128]{3,2,0,1:T(8,128)} copy(f32[1,256,32,128]{3,1,2,0:T(8,128)S(1)} %fusion.7) | data formatting | bytes 8388608 | tf_op jit(solution)/shard_map/broadcast_in_dim | solution.py:77
  132.6 6.0 %all-to-all-start.2 = ((f32[1,256,32,128]{3,2,0,1:T(8,128)}), f32[1,256,32,128]{3,2,0,1:T(8,128)}, u32[]{:S(2)}, u32[]{:S(2)}) async-start(f32[1,256,32,128]{3,2,0,1:T(8,128)} %copy.76), calls=%async_computation.2 | async-start | bytes 8388608 | tf_op jit(solution)/shard_map/all_to_all | solution.py:77
  138.5 0.7 reduce.2
  139.3 0.2 reshape.118
  139.6 0.7 reduce.4
  140.8 90.5 %all-to-all-done.2 = f32[1,256,32,128]{3,2,0,1:T(8,128)} async-done(((f32[1,256,32,128]{3,2,0,1:T(8,128)}), f32[1,256,32,128]{3,2,0,1:T(8,128)}, u32[]{:S(2)}, u32[]{:S(2)}) %all-to-all-start.2) | async-done | bytes 4194336 | tf_op jit(solution)/shard_map/all_to_all | solution.py:77
  231.3 3.9 %fusion.6 = f32[32,32,128]{2,0,1:T(8,128)S(1)} fusion(f32[8,32,32,128]{3,2,1,0:T(8,128)} %bitcast.10, f32[8,32,32]{1,0,2:T(8,128)S(1)} %get-tuple-element.6), kind=kLoop, calls=%fused_computation.10 | loop fusion | flops 1966080 | bytes 4751360 | tf_op jit(solution)/shard_map/reduce_sum | solution.py:83
  235.4 0.2 stack.3
  235.7 51.8 %all_to_all.92 = bf16[8,32,4096]{2,1,0:T(8,128)(2,1)S(1)} all-to-all(bf16[8,32,4096]{2,1,0:T(8,128)(2,1)S(1)} %stack.3), channel_id=1, replica_groups=mesh['ctx'=8,'head'=4] {'ctx'}, dimensions={0} | all-to-all | bytes 4194304 | tf_op jit(solution)/shard_map/all_to_all | solution.py:92
  287.5 28.5 %all_to_all.93 = bf16[4,64,4096]{2,1,0:T(8,128)(2,1)S(1)} all-to-all(bf16[4,64,4096]{2,1,0:T(8,128)(2,1)S(1)} %bitcast.65), channel_id=1, replica_groups=mesh['ctx'=8,'head'=4] {'head'}, dimensions={0} | all-to-all | bytes 4194304 | tf_op jit(solution)/shard_map/all_to_all | solution.py:94
  316.0 1.5 copy.89
  (31 shorter events, 1.4 us)
Async XLA Ops:
  0.0 58.0 %copy-start = (bf16[512,512]{1,0:T(8,128)(2,1)S(1)}, bf16[512,512]{1,0:T(8,128)(2,1)}, u32[]{:S(2)}) copy-start(bf16[512,512]{1,0:T(8,128)(2,1)} %param.10) | copy-start | bytes 1572868
  2.4 18.7 %all-to-all-start.1 = ((bf16[64,4,2048]{2,0,1:T(8,128)(2,1)}), bf16[64,4,2048]{2,0,1:T(8,128)(2,1)S(1)}, u32[]{:S(2)}, u32[]{:S(2)}) async-start(bf16[64,4,2048]{2,0,1:T(8,128)(2,1)} %bitcast.63), calls=%async_computation.1 | async-start | bytes 2097152 | tf_op jit(solution)/shard_map/all_to_all | solution.py:22
  6.7 18.9 %copy-start.5 = (s32[32,2]{0,1:T(2,128)S(1)}, s32[32,2]{0,1:T(2,128)}, u32[]{:S(2)}) copy-start(s32[32,2]{0,1:T(2,128)} %param.15) | copy-start | bytes 772
  6.7 18.9 %copy-start.4 = (s32[32,2,16]{0,2,1:T(8,128)S(1)}, s32[32,2,16]{0,2,1:T(8,128)}, u32[]{:S(2)}) copy-start(s32[32,2,16]{0,2,1:T(8,128)} %param.14) | copy-start | bytes 12292
  21.1 8.9 %copy-start.2 = (bf16[64,4,2048]{2,0,1:T(8,128)(2,1)}, bf16[64,4,2048]{2,0,1:T(8,128)(2,1)S(1)}, u32[]{:S(2)}) copy-start(bf16[64,4,2048]{2,0,1:T(8,128)(2,1)S(1)} %all-to-all-done.1) | copy-start | bytes 3145732
  21.1 34.8 %all-to-all-start = ((bf16[64,4,4096]{2,0,1:T(8,128)(2,1)}), bf16[64,4,4096]{2,0,1:T(8,128)(2,1)}, u32[]{:S(2)}, u32[]{:S(2)}) async-start(bf16[64,4,4096]{2,0,1:T(8,128)(2,1)} %bitcast.62), calls=%async_computation | async-start | bytes 4194304 | tf_op jit(solution)/shard_map/all_to_all | solution.py:21
  30.0 17.9 %copy-start.3 = (bf16[64,512]{1,0:T(8,128)(2,1)S(1)}, bf16[64,512]{1,0:T(8,128)(2,1)}, u32[]{:S(2)}) copy-start(bf16[64,512]{1,0:T(8,128)(2,1)} %param.11) | copy-start | bytes 196612
  87.8 21.2 %all-to-all-start.4 = ((f32[8,1,1024]{2,1,0:T(1,128)}), f32[8,1,1024]{2,1,0:T(1,128)S(1)}, u32[]{:S(2)}, u32[]{:S(2)}) async-start(f32[8,1,1024]{2,1,0:T(1,128)} %reshape.117), calls=%async_computation.4 | async-start | bytes 65536 | tf_op jit(solution)/shard_map/all_to_all | solution.py:78
  109.0 23.5 %all-to-all-start.3 = ((f32[8,1,1024]{2,1,0:T(1,128)}), f32[8,1,1024]{2,1,0:T(1,128)S(1)}, u32[]{:S(2)}, u32[]{:S(2)}) async-start(f32[8,1,1024]{2,1,0:T(1,128)} %reshape.115), calls=%async_computation.3 | async-start | bytes 65536 | tf_op jit(solution)/shard_map/all_to_all | solution.py:79
  132.6 98.7 %all-to-all-start.2 = ((f32[1,256,32,128]{3,2,0,1:T(8,128)}), f32[1,256,32,128]{3,2,0,1:T(8,128)}, u32[]{:S(2)}, u32[]{:S(2)}) async-start(f32[1,256,32,128]{3,2,0,1:T(8,128)} %copy.76), calls=%async_computation.2 | async-start | bytes 8388608 | tf_op jit(solution)/shard_map/all_to_all | solution.py:77
  287.5 30.0 %copy-start.1 = (bf16[512,512]{1,0:T(8,128)(2,1)S(1)}, bf16[512,512]{1,0:T(8,128)(2,1)}, u32[]{:S(2)}) copy-start(bf16[512,512]{1,0:T(8,128)(2,1)} %param.10) | copy-start | bytes 1572868
